TPU v7x, 128 devices: a whole 4x4x4 slice. The times are simulated.
128 devices in a mesh: scen: 32 (over y, x, z_lo), grp: 4 (over z_hi, core).
Axes of the slice: x: 4, y: 4, z: 4 (z_hi: 2, z_lo: 2; z = z_hi * 2 + z_lo), core: 2. Of those that a mesh axis runs over, the one named last changes fastest.
Arguments:
- coupling: bfloat16 [128, 768, 4096], P(('scen', 'grp')), may hold values from -6 to 6
- scen_kkt: bfloat16 [128, 768, 768], P(('scen', 'grp')), may hold values from -3 to 5, as said below
- active_rows: int32 [128], P(('scen', 'grp')), may hold values from 128 to 768, as said below
- first_hess: float32 [512], replicated, may hold values from 20 to 400
Outputs:
- factor_panels: float32 [4096, 512], P('scen')
Inputs may be any that keep to these rules, and one draw needn't show every extreme that they name: `scen_kkt`: each block is symmetric positive definite: a Gram matrix of 768 columns divided by 768 plus a positive diagonal. `active_rows`: each count is a multiple of 128; some scenario has 768 and some has 128.
All inputs are finite; a program needn't handle non-finite values.
Results may differ from a plain program's by a relative error of at most 0.0011.
Values sent between devices are 32-bit elements; how exact they have to be, the bound alone decides.
A program may use at most 64 MiB of HBM per device.

v0:
```python
import jax
import jax.numpy as jnp
from jax import lax
from jax.experimental import pallas as pl
from jax.experimental.pallas import tpu as pltpu
from jax.sharding import PartitionSpec as P

PW = 256
NC = 4096
NB = 768
F32 = jnp.float32
HIGHEST = lax.Precision.HIGHEST
MESH = pl.DeviceIdType.MESH

ORDERS = (("x", "y", "z"), ("y", "z", "x"), ("z", "x", "y"))
MAIN_N = (5, 5, 6)
MAIN_OFF = (0, 5, 10)
TOP_N = (2, 2, 1)
TOP_OFF = (0, 32, 64)


def total(terms):
    while len(terms) > 1:
        terms = [terms[i] + terms[i + 1] if i + 1 < len(terms) else terms[i] for i in range(0, len(terms), 2)]
    return terms[0]

def inverse_factor(z):
    shape = (8, 128)
    lane = lax.broadcasted_iota(jnp.int32, shape, 1)
    sub = lax.broadcasted_iota(jnp.int32, shape, 0)
    z = list(z)
    for j in range(16):
        lo = 8 * j
        zj = z[j]
        col = [jnp.broadcast_to(zj[:, lo + c : lo + c + 1], shape) for c in range(8)]
        e = {(r, c): jnp.broadcast_to(col[c][r : r + 1], shape) for c in range(8) for r in range(c, 8)}
        inv, l, t = {}, {}, {}
        for c in range(8):
            inv[c] = lax.rsqrt(e[c, c])
            for r in range(c + 1, 8):
                l[r, c] = e[r, c] * inv[c]
            for r in range(c + 1, 8):
                for q in range(c + 1, r + 1):
                    e[r, q] = e[r, q] - l[r, c] * l[q, c]
        for c in range(8):
            t[c, c] = inv[c]
            for r in range(c + 1, 8):
                t[r, c] = -inv[r] * total([l[r, m] * t[m, c] for m in range(c, r)])
        panel = (lane >= lo) & (lane < lo + 8)
        zp = jnp.where(panel, jnp.where(lane - lo == sub, 1.0, 0.0), zj)
        zb = [jnp.broadcast_to(zp[c : c + 1], shape) for c in range(8)]
        u = [total([t[r, c] * zb[c] for c in range(r + 1)]) for r in range(8)]
        w = [total([t[c, r] * u[c] for c in range(r, 8)]) for r in range(8)]
        row = u[0]
        for r in range(1, 8):
            row = jnp.where(sub == r, u[r], row)
        z[j] = jnp.where(lane < lo + 8, row, 0.0)
        for i in range(j + 1, 16):
            zi = z[i]
            q = [jnp.broadcast_to(zi[:, lo + c : lo + c + 1], shape) * w[c] for c in range(8)]
            z[i] = jnp.where(panel, 0.0, zi) - total(q)
    return z

def dot(a, b):
    return jnp.dot(a, b, precision=HIGHEST, preferred_element_type=F32)

def dot_t(a, b):
    return lax.dot_general(a, b, (((0,), (0,)), ((), ())), precision=HIGHEST, preferred_element_type=F32)

def solve_kernel(act_ref, k_ref, c_ref, st_ref, aug, linv, xs):
    row = lax.broadcasted_iota(jnp.int32, (NB, 1), 0)
    keep = (row < act_ref[0]).astype(F32)
    aug[:, :NB] = k_ref[...].astype(F32)
    aug[:, NB:] = c_ref[...].astype(F32) * keep

    def step(j, _):
        at = pl.multiple_of(j * 128, 128)
        rows = pl.ds(at, 128)
        z = [aug[pl.ds(at + 8 * i, 8), pl.ds(at, 128)] for i in range(16)]
        z = inverse_factor(z)
        for i in range(16):
            linv[j, 8 * i : 8 * i + 8, :] = z[i]
        y = dot(linv[j], aug[rows, :])
        aug[rows, :] = y

        def update(i, _):
            ai = pl.multiple_of(i * 128, 128)
            g = aug[rows, pl.ds(ai, 128)]
            below = pl.ds(ai, 128)
            aug[below, :] = aug[below, :] - dot_t(g, aug[rows, :])
            return 0

        lax.fori_loop(j + 1, NB // 128, update, 0)
        return 0

    lax.fori_loop(0, NB // 128, step, 0)
    for j in range(NB // 128 - 1, -1, -1):
        lo, hi = j * 128, j * 128 + 128
        acc = aug[lo:hi, NB:]
        if hi < NB:
            acc = acc - dot(aug[lo:hi, hi:NB], xs[hi:, :])
        x = dot_t(linv[j], acc)
        xs[lo:hi, :] = x
        st_ref[:, lo:hi] = (x * keep[lo:hi]).T.astype(jnp.bfloat16)

def scenario_solve(active, kkt, coupling):
    vspec = pl.BlockSpec(memory_space=pltpu.VMEM)
    return pl.pallas_call(
        solve_kernel,
        grid=(1,),
        in_specs=[pl.BlockSpec(memory_space=pltpu.SMEM), pl.BlockSpec((NB, NB), lambda i: (0, 0)),
                  pl.BlockSpec((NB, 512), lambda i: (0, 0))],
        out_specs=pl.BlockSpec((512, NB), lambda i: (0, 0)),
        out_shape=jax.ShapeDtypeStruct((512, NB), jnp.bfloat16),
        scratch_shapes=[pltpu.VMEM((NB, 1280), F32), pltpu.VMEM((6, 128, 128), F32), pltpu.VMEM((NB, 512), F32)],
        compiler_params=pltpu.CompilerParams(vmem_limit_bytes=48 << 20),
    )(active, kkt, coupling)


def product_kernel(st_ref, c_ref, main_ref, top_ref, keep_ref):
    step = pl.program_id(0)
    res = jnp.dot(st_ref[...], c_ref[...], preferred_element_type=F32)
    for t in range(4):
        y, x, zl = step // 2, (step % 2) * 2 + t // 2, t % 2
        part = res[:, t * 128 : (t + 1) * 128]
        for q in range(4):
            zh, c = q // 2, q % 2
            pos = {"x": x, "y": y, "z": 2 * zh + zl}
            for k in range(3):
                d0, d1, d2 = ORDERS[k]
                n = MAIN_N[k]
                idx = MAIN_OFF[k] * 64 + ((pos[d0] * 4 + pos[d1]) * 4 + pos[d2]) * n
                lo = q * 128 + MAIN_OFF[k] * 8
                main_ref[c, pl.ds(idx, n)] = part[lo : lo + 8 * n].reshape(n, 8, 128)

    @pl.when(step == 0)
    def _():
        keep_ref[...] = res

        def block(a, s):
            return keep_ref[a * 128 : (a + 1) * 128, s * 128 : (s + 1) * 128]

        def put(i, v):
            top_ref[i // 5, pl.ds((i % 5) * 16, 16)] = v.reshape(16, 8, 128)

        for base, (p, r) in ((0, (0, 1)), (7, (2, 3))):
            put(base, 0.5 * (block(p, p) + block(p, p).T))
            put(base + 1, 0.5 * (block(p, r) + block(r, p).T))
            put(base + 2, 0.5 * (block(r, r) + block(r, r).T))
        put(3, block(0, 2))
        put(4, block(1, 2))
        put(5, block(0, 3))
        put(6, block(1, 3))


def product(solved_t, coupling):
    return pl.pallas_call(
        product_kernel,
        grid=(8,),
        in_specs=[
            pl.BlockSpec((512, NB), lambda i: (0, 0)),
            pl.BlockSpec((NB, 512), lambda i: (0, i)),
        ],
        out_specs=[
            pl.BlockSpec((2, 1024, 8, 128), lambda i: (0, 0, 0, 0)),
            pl.BlockSpec((2, 80, 8, 128), lambda i: (0, 0, 0, 0)),
        ],
        out_shape=[
            jax.ShapeDtypeStruct((2, 1024, 8, 128), F32),
            jax.ShapeDtypeStruct((2, 80, 8, 128), F32),
        ],
        scratch_shapes=[pltpu.VMEM((512, 512), F32)],
        compiler_params=pltpu.CompilerParams(vmem_limit_bytes=48 << 20),
    )(solved_t, coupling)


def exchange_kernel(
    main_ref, top_ref, own_ref, all_ref,
    acc, ra, r0, r1, r2, own, tacc, ta, t0, t1, t2, gat,
    core_s, core_r, st_s, st_r, tst_s, tst_r, ag_s, ag_r,
):
    si = lax.axis_index("scen")
    gi = lax.axis_index("grp")
    c = gi % 2
    zh = gi // 2
    pos = {"y": si // 8, "x": (si // 2) % 4, "z": 2 * zh + si % 2}

    def device(y, x, z, core):
        return {"scen": (y * 4 + x) * 2 + z % 2, "grp": (z // 2) * 2 + core}

    def peer(axis, dist):
        at = dict(pos)
        at[axis] = (at[axis] + dist) % 4
        return device(at["y"], at["x"], at["z"], c)

    partner = device(pos["y"], pos["x"], pos["z"], 1 - c)
    far = device(pos["y"], pos["x"], (pos["z"] + 2) % 4, 1 - c)

    barrier = pltpu.get_barrier_semaphore()
    greet = [peer(a, d) for a in "xyz" for d in (1, 2, 3)] + [partner, far]
    for dev in greet:
        pl.semaphore_signal(barrier, inc=1, device_id=dev, device_id_type=MESH)
    pl.semaphore_wait(barrier, len(greet))

    pending = []

    def send(src, dst, ssem, rsem, dev):
        cp = pltpu.make_async_remote_copy(
            src_ref=src, dst_ref=dst, send_sem=ssem, recv_sem=rsem,
            device_id=dev, device_id_type=MESH,
        )
        cp.start()
        pending.append(cp)
        return cp

    tcore = send(top_ref.at[1 - c], ta, core_s.at[0], core_r.at[0], partner)
    mcore = []
    for k in range(3):
        sl = pl.ds(MAIN_OFF[k] * 64, MAIN_N[k] * 64)
        mcore.append(
            send(main_ref.at[1 - c, sl], ra.at[sl], core_s.at[1 + k], core_r.at[1 + k], partner)
        )

    tcore.wait_recv()
    tacc[...] = top_ref[c] + ta[...]

    def scatter(buf, base, n, axis, slots, off, ssem, rsem, first):
        out = []
        for d in (1, 2, 3):
            p = (pos[axis] + d) % 4
            out.append(
                send(
                    buf.at[pl.ds(base + p * n, n)], slots.at[d - 1, pl.ds(off, n)],
                    ssem.at[first + d - 1], rsem.at[first + d - 1], peer(axis, d),
                )
            )
        return out

    def gather_sum(buf, base, n, slots, off, copies):
        for cp in copies:
            cp.wait_recv()
        own_piece = pl.ds(base, n)
        sl = pl.ds(off, n)
        buf[own_piece] = buf[own_piece] + slots[0, sl] + slots[1, sl] + slots[2, sl]

    base = list(TOP_OFF)
    for stage, slots in ((0, t0), (1, t1)):
        flights = []
        for k in range(3):
            n = TOP_N[k] * (4 if stage == 0 else 1)
            off = TOP_OFF[k] // 4 if stage == 0 else TOP_OFF[k] // 16
            axis = ORDERS[k][stage]
            flights.append(
                scatter(tacc, base[k], n, axis, slots, off, tst_s, tst_r, (stage * 3 + k) * 3)
            )
        for k in range(3):
            n = TOP_N[k] * (4 if stage == 0 else 1)
            off = TOP_OFF[k] // 4 if stage == 0 else TOP_OFF[k] // 16
            base[k] = base[k] + pos[ORDERS[k][stage]] * n
            gather_sum(tacc, base[k], n, slots, off, flights[k])
    flights = []
    for k in range(3):
        n, off = TOP_N[k], TOP_OFF[k] // 16
        axis = ORDERS[k][2]
        flights.append([
            send(
                tacc.at[pl.ds(base[k], n)], t2.at[d - 1, pl.ds(off, n)],
                tst_s.at[(6 + k) * 3 + d - 1], tst_r.at[(6 + k) * 3 + d - 1], peer(axis, d),
            )
            for d in (1, 2, 3)
        ])
    for k in range(3):
        n, off = TOP_N[k], TOP_OFF[k] // 16
        for cp in flights[k]:
            cp.wait_recv()
        mine = pos[ORDERS[k][2]]
        parts = [tacc[pl.ds(base[k], n)]] + [t2[d, pl.ds(off, n)] for d in range(3)]
        total = None
        for p in range(4):
            dist = (mine - p) % 4
            v = jnp.where(
                dist == 0, parts[0],
                jnp.where(dist == 1, parts[1], jnp.where(dist == 2, parts[2], parts[3])),
            )
            total = v if total is None else total + v
        gat[c, pl.ds(base[k], n)] = total
    for stage in (1, 0):
        flights = []
        for k in range(3):
            n = TOP_N[k] * (1 if stage == 1 else 4)
            if stage == 0:
                base[k] = base[k] - pos[ORDERS[k][1]] * TOP_N[k]
            piece = gat.at[c, pl.ds(base[k], n)]
            first = ((1 - stage) * 3 + k) * 3
            flights.append([
                send(piece, piece, ag_s.at[first + d - 1], ag_r.at[first + d - 1],
                     peer(ORDERS[k][stage], d))
                for d in (1, 2, 3)
            ])
        for k in range(3):
            for cp in flights[k]:
                cp.wait_recv()
    last = send(gat.at[c], gat.at[c], ag_s.at[18], ag_r.at[18], partner)

    base = [MAIN_OFF[k] * 64 for k in range(3)]
    flights = []
    for k in range(3):
        mcore[k].wait_recv()
        sl = pl.ds(MAIN_OFF[k] * 64, MAIN_N[k] * 64)
        acc[sl] = main_ref[c, sl] + ra[sl]
        flights.append(
            scatter(acc, base[k], 16 * MAIN_N[k], ORDERS[k][0], r0, MAIN_OFF[k] * 16,
                    st_s, st_r, k * 3)
        )
    for stage, slots, m in ((0, r0, 16), (1, r1, 4), (2, r2, 1)):
        following = []
        for k in range(3):
            n = MAIN_N[k] * m
            base[k] = base[k] + pos[ORDERS[k][stage]] * n
            gather_sum(acc, base[k], n, slots, MAIN_OFF[k] * m, flights[k])
            if stage < 2:
                following.append(
                    scatter(acc, base[k], n // 4, ORDERS[k][stage + 1], (r1, r2)[stage],
                            MAIN_OFF[k] * (m // 4), st_s, st_r, ((stage + 1) * 3 + k) * 3)
                )
        flights = following
    for k in range(3):
        own[gi, pl.ds(MAIN_OFF[k], MAIN_N[k])] = acc[pl.ds(base[k], MAIN_N[k])]
    mine = own.at[gi]
    flights = [
        send(mine, mine, ag_s.at[19 + j], ag_r.at[19 + j], dev)
        for j, dev in enumerate((partner, peer("z", 2), far))
    ]
    for cp in flights:
        cp.wait_recv()
    own_ref[...] = own[...]
    last.wait_recv()
    all_ref[...] = gat[...]
    for cp in pending:
        cp.wait_send()


def exchange(main, top):
    tile = (8, 128)
    vm = lambda *lead: pltpu.VMEM(lead + tile, F32)
    sem = lambda n: pltpu.SemaphoreType.DMA((n,))
    vspec = pl.BlockSpec(memory_space=pltpu.VMEM)
    return pl.pallas_call(
        exchange_kernel,
        in_specs=[vspec, vspec],
        out_specs=[vspec, vspec],
        out_shape=[
            jax.ShapeDtypeStruct((4, 16) + tile, F32),
            jax.ShapeDtypeStruct((2, 80) + tile, F32),
        ],
        scratch_shapes=[
            vm(1024), vm(1024), vm(3, 256), vm(3, 64), vm(3, 16), vm(4, 16),
            vm(80), vm(80), vm(3, 20), vm(3, 5), vm(3, 5), vm(2, 80),
            sem(4), sem(4), sem(27), sem(27), sem(27), sem(27), sem(22), sem(22),
        ],
        compiler_params=pltpu.CompilerParams(
            collective_id=0, has_side_effects=True, vmem_limit_bytes=48 << 20
        ),
    )(main, top)


UPPER = ((0, 0), (0, 1), (1, 1), (0, 2), (1, 2), (0, 3), (1, 3), (2, 2), (2, 3), (3, 3))


def panel_kernel(hess_ref, own_ref, all_ref, out_ref, aug, linv):
    si = lax.axis_index("scen")
    row = lax.broadcasted_iota(jnp.int32, (128, 128), 0)
    lane = lax.broadcasted_iota(jnp.int32, (128, 128), 1)
    for i, (a, b) in enumerate(UPPER):
        v = all_ref[i // 5, pl.ds((i % 5) * 16, 16)].reshape(128, 128)
        if a == b:
            v = v + jnp.where(row == lane, hess_ref[a : a + 1, :], 0.0)
        aug[a * 128 : (a + 1) * 128, b * 128 : (b + 1) * 128] = v
    aug[:, 512:] = own_ref[...].reshape(512, 128)

    def step(j, _):
        at = pl.multiple_of(j * 128, 128)
        rows = pl.ds(at, 128)
        z = [aug[pl.ds(at + 8 * i, 8), pl.ds(at, 128)] for i in range(16)]
        z = inverse_factor(z)
        for i in range(16):
            linv[8 * i : 8 * i + 8, :] = z[i]
        aug[rows, :] = dot(linv[...], aug[rows, :])

        def update(i, _):
            ai = pl.multiple_of(i * 128, 128)
            below = pl.ds(ai, 128)
            aug[below, :] = aug[below, :] - dot_t(aug[rows, pl.ds(ai, 128)], aug[rows, :])
            return 0

        lax.fori_loop(j + 1, 4, update, 0)
        return 0

    lax.fori_loop(0, 4, step, 0)
    at = pl.multiple_of(jnp.where(si < 4, si, 4) * 128, 128)
    for j in range(4):
        v = aug[j * 128 : (j + 1) * 128, pl.ds(at, 128)]
        v = jnp.where(j * 128 + row <= si * 128 + lane, v, 0.0)
        out_ref[:, j * 128 : (j + 1) * 128] = v.T


def panel(hess, own, gathered):
    vspec = pl.BlockSpec(memory_space=pltpu.VMEM)
    return pl.pallas_call(
        panel_kernel,
        in_specs=[vspec, vspec, vspec],
        out_specs=vspec,
        out_shape=jax.ShapeDtypeStruct((128, 512), F32),
        scratch_shapes=[pltpu.VMEM((512, 640), F32), pltpu.VMEM((128, 128), F32)],
        compiler_params=pltpu.CompilerParams(vmem_limit_bytes=16 << 20),
    )(hess, own, gathered)


def per_device(coupling, scen_kkt, active_rows, first_hess):
    solved_t = scenario_solve(active_rows, scen_kkt[0], coupling[0])
    main, top = product(solved_t, coupling[0])
    own, gathered = exchange(main, top)
    return panel(first_hess.reshape(4, 128), own, gathered)


def solution(mesh):
    placed = (
        P(("scen", "grp"), None, None),
        P(("scen", "grp"), None, None),
        P(("scen", "grp")),
        P(),
    )
    return jax.shard_map(
        per_device, mesh=mesh, in_specs=placed, out_specs=P("scen", None), check_vma=False
    )
```

profile of v0, /device:TPU:0, one launch (start us, length us, event | category | flops | bytes accessed | tf_op | source)
XLA Modules:
  0.0 157.5 jit_solution(17555245078084251439)
XLA Ops:
  0.7 0.0 copy-start
  0.7 1.3 copy-done
  1.9 53.4 %shard_map.46.st_ref = bf16[512,768]{1,0:T(8,128)(2,1)S(1)} custom-call(s32[1]{0:T(128)S(6)} %copy.5.act_ref, bf16[768,768]{1,0:T(8,128)(2,1)S(1)} %bitcast.3, bf16[768,4096]{1,0:T(8,128)(2,1)} %bitcast.5), custom_call_target="tpu_custom_call" | custom-call | tf_op jit(solution)/shard_map/pallas_call | solution.py:108
  55.3 11.3 %shard_map.47 = (f32[2,1024,8,128]{3,2,1,0:T(8,128)}, f32[2,80,8,128]{3,2,1,0:T(8,128)S(1)}) custom-call(bf16[512,768]{1,0:T(8,128)(2,1)S(1)} %shard_map.46.st_ref, bf16[768,4096]{1,0:T(8,128)(2,1)} %bitcast.6), custom_call_target="tpu_custom_call" | custom-call | tf_op jit(solution)/shard_map/pallas_call | solution.py:157
  66.6 0.0 copy-start.1
  66.6 64.9 %shard_map.48 = (f32[4,16,8,128]{3,2,1,0:T(8,128)S(1)}, f32[2,80,8,128]{3,2,1,0:T(8,128)S(1)}) custom-call(f32[2,1024,8,128]{3,2,1,0:T(8,128)} %get-tuple-element.9.main_ref, f32[2,80,8,128]{3,2,1,0:T(8,128)S(1)} %get-tuple-element.10.top_ref), custom_call_target="tpu_custom_call" | custom-call | tf_op jit(solution)/shard_map/pallas_call | solution.py:348
  131.5 0.0 copy-done.1
  131.5 25.9 %shard_map.49 = f32[128,512]{1,0:T(8,128)} custom-call(f32[4,128]{1,0:T(4,128)S(1)} %bitcast.4, f32[4,16,8,128]{3,2,1,0:T(8,128)S(1)} %get-tuple-element.11.own_ref, f32[2,80,8,128]{3,2,1,0:T(8,128)S(1)} %get-tuple-element.12.all_ref), custom_call_target="tpu_custom_call" | custom-call | tf_op jit(solution)/shard_map/pallas_call | solution.py:409
Async XLA Ops:
  0.7 1.3 copy-start
  66.6 64.9 %copy-start.1 = (f32[512]{0:T(512)S(1)}, f32[512]{0:T(512)}, u32[]{:S(2)}) copy-start(f32[512]{0:T(512)} %param.7) | copy-start | bytes 6148
where the time goes:
time: 159 us; the launch traced here: 157 us
  Pallas kernels  156 us (98%)
    pallas_call x1, Pallas kernels, exchange(): pl.pallas_call(exchange_kernel, in_specs=[vspec, vspec], out_specs=[vspec...  64.9 us
    pallas_call x1, Pallas kernels, scenario_solve(): pl.pallas_call(solve_kernel, grid=(1,), in_specs=[pl.BlockSpec(memory_spa...  53.4 us
    pallas_call x1, Pallas kernels, panel(): pl.pallas_call(panel_kernel, in_specs=[vspec, vspec, vspec], out_specs=vs...  25.9 us
    pallas_call x1, Pallas kernels, product(): pl.pallas_call(product_kernel, grid=(8,), in_specs=[pl.BlockSpec((512, NB...  11.3 us

commit v1 on v0

v1 whole, which is shorter than its diff:
```python
import jax
import jax.numpy as jnp
from jax import lax
from jax.experimental import pallas as pl
from jax.experimental.pallas import tpu as pltpu
from jax.sharding import PartitionSpec as P

PW = 256
NC = 4096
NB = 768
F32 = jnp.float32
HIGHEST = lax.Precision.HIGHEST
MESH = pl.DeviceIdType.MESH

ORDERS = (("x", "y", "z"), ("y", "z", "x"), ("z", "x", "y"))
MAIN_N = (5, 5, 6)
MAIN_OFF = (0, 5, 10)
TOP_N = (2, 2, 1)
TOP_OFF = (0, 32, 64)


def total(terms):
    while len(terms) > 1:
        terms = [terms[i] + terms[i + 1] if i + 1 < len(terms) else terms[i] for i in range(0, len(terms), 2)]
    return terms[0]

def inverse_factor(z):
    shape = (8, 128)
    lane = lax.broadcasted_iota(jnp.int32, shape, 1)
    sub = lax.broadcasted_iota(jnp.int32, shape, 0)
    z = list(z)
    for j in range(16):
        lo = 8 * j
        zj = z[j]
        col = [jnp.broadcast_to(zj[:, lo + c : lo + c + 1], shape) for c in range(8)]
        e = {(r, c): jnp.broadcast_to(col[c][r : r + 1], shape) for c in range(8) for r in range(c, 8)}
        inv, l, t = {}, {}, {}
        for c in range(8):
            inv[c] = lax.rsqrt(e[c, c])
            for r in range(c + 1, 8):
                l[r, c] = e[r, c] * inv[c]
            for r in range(c + 1, 8):
                for q in range(c + 1, r + 1):
                    e[r, q] = e[r, q] - l[r, c] * l[q, c]
        for c in range(8):
            t[c, c] = inv[c]
            for r in range(c + 1, 8):
                t[r, c] = -inv[r] * total([l[r, m] * t[m, c] for m in range(c, r)])
        panel = (lane >= lo) & (lane < lo + 8)
        zp = jnp.where(panel, jnp.where(lane - lo == sub, 1.0, 0.0), zj)
        zb = [jnp.broadcast_to(zp[c : c + 1], shape) for c in range(8)]
        u = [total([t[r, c] * zb[c] for c in range(r + 1)]) for r in range(8)]
        w = [total([t[c, r] * u[c] for c in range(r, 8)]) for r in range(8)]
        row = u[0]
        for r in range(1, 8):
            row = jnp.where(sub == r, u[r], row)
        z[j] = jnp.where(lane < lo + 8, row, 0.0)
        for i in range(j + 1, 16):
            zi = z[i]
            q = [jnp.broadcast_to(zi[:, lo + c : lo + c + 1], shape) * w[c] for c in range(8)]
            z[i] = jnp.where(panel, 0.0, zi) - total(q)
    return z

def dot(a, b):
    return jnp.dot(a, b, precision=HIGHEST, preferred_element_type=F32)

def dot_t(a, b):
    return lax.dot_general(a, b, (((0,), (0,)), ((), ())), precision=HIGHEST, preferred_element_type=F32)

def solve_kernel(act_ref, k_ref, c_ref, st_ref, aug, linv, xs):
    row = lax.broadcasted_iota(jnp.int32, (NB, 1), 0)
    keep = (row < act_ref[0]).astype(F32)
    aug[:, :NB] = k_ref[...].astype(F32)
    aug[:, NB:] = c_ref[...].astype(F32) * keep

    def step(j, _):
        at = pl.multiple_of(j * 128, 128)
        rows = pl.ds(at, 128)
        z = [aug[pl.ds(at + 8 * i, 8), pl.ds(at, 128)] for i in range(16)]
        z = inverse_factor(z)
        for i in range(16):
            linv[j, 8 * i : 8 * i + 8, :] = z[i]
        y = dot(linv[j], aug[rows, :])
        aug[rows, :] = y

        def update(i, _):
            ai = pl.multiple_of(i * 128, 128)
            g = aug[rows, pl.ds(ai, 128)]
            below = pl.ds(ai, 128)
            aug[below, :] = aug[below, :] - dot_t(g, aug[rows, :])
            return 0

        lax.fori_loop(j + 1, NB // 128, update, 0)
        return 0

    lax.fori_loop(0, NB // 128, step, 0)
    for j in range(NB // 128 - 1, -1, -1):
        lo, hi = j * 128, j * 128 + 128
        acc = aug[lo:hi, NB:]
        if hi < NB:
            acc = acc - dot(aug[lo:hi, hi:NB], xs[hi:, :])
        x = dot_t(linv[j], acc)
        xs[lo:hi, :] = x
        st_ref[:, lo:hi] = (x * keep[lo:hi]).T.astype(jnp.bfloat16)

def scenario_solve(active, kkt, coupling):
    vspec = pl.BlockSpec(memory_space=pltpu.VMEM)
    return pl.pallas_call(
        solve_kernel,
        grid=(1,),
        in_specs=[pl.BlockSpec(memory_space=pltpu.SMEM), pl.BlockSpec((NB, NB), lambda i: (0, 0)),
                  pl.BlockSpec((NB, 512), lambda i: (0, 0))],
        out_specs=pl.BlockSpec((512, NB), lambda i: (0, 0)),
        out_shape=jax.ShapeDtypeStruct((512, NB), jnp.bfloat16),
        scratch_shapes=[pltpu.VMEM((NB, 1280), F32), pltpu.VMEM((6, 128, 128), F32), pltpu.VMEM((NB, 512), F32)],
        compiler_params=pltpu.CompilerParams(vmem_limit_bytes=48 << 20),
    )(active, kkt, coupling)


UPPER = ((0, 0), (0, 1), (1, 1), (0, 2), (1, 2), (0, 3), (1, 3), (2, 2), (2, 3), (3, 3))


def tail_kernel(
    hess_ref, st_ref, coup_ref, out_ref,
    cbuf, ma, mb, mc, ra, rb, rc, pa, pb, pc, qa, qb, qc, last_slots, own,
    keep, top, tacc, ta, t0, t1, t2, gat, aug, linv,
    c_sem, core_s, core_r, tcore_s, tcore_r, st_s, st_r, tst_s, tst_r, ag_s, ag_r,
):
    si = lax.axis_index("scen")
    gi = lax.axis_index("grp")
    c = gi % 2
    zh = gi // 2
    pos = {"y": si // 8, "x": (si // 2) % 4, "z": 2 * zh + si % 2}
    main, recv_core = (ma, mb, mc), (ra, rb, rc)
    slots = ((pa, pb, pc), (qa, qb, qc))

    loads = [
        pltpu.make_async_copy(coup_ref.at[:, pl.ds(i * 512, 512)], cbuf.at[i], c_sem.at[i])
        for i in range(8)
    ]
    for cp in loads:
        cp.start()

    def device(y, x, z, core):
        return {"scen": (y * 4 + x) * 2 + z % 2, "grp": (z // 2) * 2 + core}

    def peer(axis, dist):
        at = dict(pos)
        at[axis] = (at[axis] + dist) % 4
        return device(at["y"], at["x"], at["z"], c)

    partner = device(pos["y"], pos["x"], pos["z"], 1 - c)
    far = device(pos["y"], pos["x"], (pos["z"] + 2) % 4, 1 - c)

    barrier = pltpu.get_barrier_semaphore()
    greet = [peer(a, d) for a in "xyz" for d in (1, 2, 3)] + [partner, far]
    for dev in greet:
        pl.semaphore_signal(barrier, inc=1, device_id=dev, device_id_type=MESH)
    pl.semaphore_wait(barrier, len(greet))

    pending = []

    def send(src, dst, ssem, rsem, dev):
        cp = pltpu.make_async_remote_copy(
            src_ref=src, dst_ref=dst, send_sem=ssem, recv_sem=rsem,
            device_id=dev, device_id_type=MESH,
        )
        cp.start()
        pending.append(cp)
        return cp

    chunk_flights = []

    def region(k, y, x0):
        at = {"x": pl.ds(x0, 2), "y": y, "z": pl.ds(0, 4)}
        return tuple(at[a] for a in ORDERS[k])

    def chunk(i):
        y, x0 = i // 2, (i % 2) * 2
        loads[i].wait()
        res = jnp.dot(st_ref[...], cbuf[i], preferred_element_type=F32)
        if i == 0:
            keep[...] = res
        for t in range(4):
            x, zl = x0 + t // 2, t % 2
            part = res[:, t * 128 : (t + 1) * 128]
            for q in range(4):
                at = {"x": x, "y": y, "z": 2 * (q // 2) + zl}
                for k in range(3):
                    n = MAIN_N[k]
                    lo = q * 128 + MAIN_OFF[k] * 8
                    i0, i1, i2 = (at[a] for a in ORDERS[k])
                    main[k][q % 2, i0, i1, i2] = part[lo : lo + 8 * n].reshape(n, 8, 128)

    def chunk_send(i):
        y, x0 = i // 2, (i % 2) * 2
        out = []
        for k in range(3):
            r = region(k, y, x0)
            out.append(
                send(main[k].at[(1 - c,) + r], recv_core[k].at[r],
                     core_s.at[i * 3 + k], core_r.at[i * 3 + k], partner)
            )
        chunk_flights.append(out)

    def chunk_add(i):
        y, x0 = i // 2, (i % 2) * 2
        for k in range(3):
            chunk_flights[i][k].wait_recv()
            r = region(k, y, x0)
            main[k][(c,) + r] = main[k][(c,) + r] + recv_core[k][r]

    def top_tiles():
        def block(a, s):
            return keep[a * 128 : (a + 1) * 128, s * 128 : (s + 1) * 128]

        def put(i, v):
            top[i // 5, pl.ds((i % 5) * 16, 16)] = v.reshape(16, 8, 128)

        for base, (p, r) in ((0, (0, 1)), (7, (2, 3))):
            put(base, 0.5 * (block(p, p) + block(p, p).T))
            put(base + 1, 0.5 * (block(p, r) + block(r, p).T))
            put(base + 2, 0.5 * (block(r, r) + block(r, r).T))
        put(3, block(0, 2))
        put(4, block(1, 2))
        put(5, block(0, 3))
        put(6, block(1, 3))

    tbase = list(TOP_OFF)
    tflights = [[], [], []]

    def top_n(k, stage):
        return (TOP_N[k] * 4, TOP_N[k], TOP_N[k])[stage]

    def top_off(k, stage):
        return (TOP_OFF[k] // 4, TOP_OFF[k] // 16, TOP_OFF[k] // 16)[stage]

    def top_scatter(stage):
        dst = (t0, t1)[stage]
        for k in range(3):
            n, off, axis = top_n(k, stage), top_off(k, stage), ORDERS[k][stage]
            first = (stage * 3 + k) * 3
            tflights[k] = [
                send(tacc.at[pl.ds(tbase[k] + (pos[axis] + d) % 4 * n, n)],
                     dst.at[d - 1, pl.ds(off, n)],
                     tst_s.at[first + d - 1], tst_r.at[first + d - 1], peer(axis, d))
                for d in (1, 2, 3)
            ]

    def top_sum(stage):
        src = (t0, t1)[stage]
        for k in range(3):
            n, off, axis = top_n(k, stage), top_off(k, stage), ORDERS[k][stage]
            for cp in tflights[k]:
                cp.wait_recv()
            tbase[k] = tbase[k] + pos[axis] * n
            mine, sl = pl.ds(tbase[k], n), pl.ds(off, n)
            tacc[mine] = tacc[mine] + src[0, sl] + src[1, sl] + src[2, sl]

    def top_share():
        for k in range(3):
            n, off, axis = top_n(k, 2), top_off(k, 2), ORDERS[k][2]
            first = (6 + k) * 3
            tflights[k] = [
                send(tacc.at[pl.ds(tbase[k], n)], t2.at[d - 1, pl.ds(off, n)],
                     tst_s.at[first + d - 1], tst_r.at[first + d - 1], peer(axis, d))
                for d in (1, 2, 3)
            ]

    def top_total():
        for k in range(3):
            n, off = top_n(k, 2), top_off(k, 2)
            for cp in tflights[k]:
                cp.wait_recv()
            mine = pos[ORDERS[k][2]]
            parts = [tacc[pl.ds(tbase[k], n)]] + [t2[d, pl.ds(off, n)] for d in range(3)]
            vals = []
            for p in range(4):
                dist = (mine - p) % 4
                vals.append(jnp.where(
                    dist == 0, parts[0],
                    jnp.where(dist == 1, parts[1], jnp.where(dist == 2, parts[2], parts[3])),
                ))
            gat[c, pl.ds(tbase[k], n)] = (vals[0] + vals[1]) + (vals[2] + vals[3])

    def top_gather(stage):
        for k in range(3):
            n = TOP_N[k] * (1 if stage == 1 else 4)
            if stage == 0:
                tbase[k] = tbase[k] - pos[ORDERS[k][1]] * TOP_N[k]
            piece = gat.at[c, pl.ds(tbase[k], n)]
            first = ((1 - stage) * 3 + k) * 3
            tflights[k] = [
                send(piece, piece, ag_s.at[first + d - 1], ag_r.at[first + d - 1],
                     peer(ORDERS[k][stage], d))
                for d in (1, 2, 3)
            ]

    def top_wait():
        for k in range(3):
            for cp in tflights[k]:
                cp.wait_recv()

    def where(k, stage):
        return (c,) + tuple(pos[a] for a in ORDERS[k][:stage])

    def row_copy(stage, k, d):
        axis = ORDERS[k][stage]
        src = main[k].at[where(k, stage) + ((pos[axis] + d) % 4,)]
        dst = last_slots.at[d - 1, pl.ds(MAIN_OFF[k], MAIN_N[k])] if stage == 2 else slots[stage][k].at[d - 1]
        i = (stage * 3 + k) * 3 + d - 1
        return pltpu.make_async_remote_copy(
            src_ref=src, dst_ref=dst, send_sem=st_s.at[i], recv_sem=st_r.at[i],
            device_id=peer(axis, d), device_id_type=MESH,
        )

    def row_scatter(stage, k):
        for d in (1, 2, 3):
            row_copy(stage, k, d).start()

    def row_sum(stage, k):
        for d in (1, 2, 3):
            row_copy(stage, k, d).wait_recv()
        at = where(k, stage + 1)
        got = [
            last_slots[d, pl.ds(MAIN_OFF[k], MAIN_N[k])] if stage == 2 else slots[stage][k][d]
            for d in range(3)
        ]
        total_rows = (main[k][at] + got[0]) + (got[1] + got[2])
        if stage == 2:
            own[gi, pl.ds(MAIN_OFF[k], MAIN_N[k])] = total_rows
        else:
            main[k][at] = total_rows

    chunk(0)
    top_tiles()
    tcore = send(top.at[1 - c], ta, tcore_s, tcore_r, partner)
    chunk_send(0)
    chunk(1)
    chunk_send(1)
    tcore.wait_recv()
    tacc[...] = top[c] + ta[...]
    top_scatter(0)
    for i in (2, 3, 4):
        chunk(i)
        chunk_send(i)
    top_sum(0)
    top_scatter(1)
    for i in (5, 6, 7):
        chunk(i)
        chunk_send(i)
    top_sum(1)
    top_share()
    for i in range(8):
        chunk_add(i)
    top_total()
    top_gather(1)
    if EARLY_ROWS:
        for k in range(3):
            row_scatter(0, k)
    top_wait()
    top_gather(0)
    if not EARLY_ROWS:
        for k in range(3):
            row_scatter(0, k)
    top_wait()
    tlast = send(gat.at[c], gat.at[c], ag_s.at[18], ag_r.at[18], partner)
    tlast.wait_recv()

    row = lax.broadcasted_iota(jnp.int32, (128, 128), 0)
    lane = lax.broadcasted_iota(jnp.int32, (128, 128), 1)
    for i, (a, b) in enumerate(UPPER):
        v = gat[i // 5, pl.ds((i % 5) * 16, 16)].reshape(128, 128)
        if a == b:
            v = v + jnp.where(row == lane, hess_ref[a : a + 1, :], 0.0)
        aug[a * 128 : (a + 1) * 128, b * 128 : (b + 1) * 128] = v

    def step(j, _):
        @pl.when(j == 3)
        def _():
            for k in range(3):
                row_sum(0, k)
                row_scatter(1, k)

        at = pl.multiple_of(j * 128, 128)
        rows = pl.ds(at, 128)
        z = [aug[pl.ds(at + 8 * i, 8), pl.ds(at, 128)] for i in range(16)]
        z = inverse_factor(z)
        for i in range(16):
            linv[j, 8 * i : 8 * i + 8, :] = z[i]
        aug[rows, :] = dot(linv[j], aug[rows, :])

        def update(i, _):
            ai = pl.multiple_of(i * 128, 128)
            below = pl.ds(ai, 128)
            aug[below, :] = aug[below, :] - dot_t(aug[rows, pl.ds(ai, 128)], aug[rows, :])
            return 0

        lax.fori_loop(j + 1, 4, update, 0)
        return 0

    lax.fori_loop(0, 4, step, 0)
    for k in range(3):
        row_sum(1, k)
        row_scatter(2, k)
    for k in range(3):
        row_sum(2, k)
    mine = own.at[gi]
    flights = [
        send(mine, mine, ag_s.at[19 + j], ag_r.at[19 + j], dev)
        for j, dev in enumerate((partner, peer("z", 2), far))
    ]
    for cp in flights:
        cp.wait_recv()

    solved = []
    for j in range(4):
        acc = own[j].reshape(128, 128)
        for i in range(j):
            acc = acc - dot_t(aug[i * 128 : (i + 1) * 128, j * 128 : (j + 1) * 128], solved[i])
        solved.append(dot(linv[j], acc))
    at = pl.multiple_of(jnp.where(si < 4, si, 0) * 128, 128)
    for j in range(4):
        v = jnp.where(si < 4, aug[j * 128 : (j + 1) * 128, pl.ds(at, 128)], solved[j])
        v = jnp.where(j * 128 + row <= si * 128 + lane, v, 0.0)
        out_ref[:, j * 128 : (j + 1) * 128] = v.T
    for cp in pending:
        cp.wait_send()
    for stage in range(3):
        for k in range(3):
            for d in (1, 2, 3):
                row_copy(stage, k, d).wait_send()


EARLY_ROWS = True


def tail(hess, solved_t, coupling):
    tile = (8, 128)
    vm = lambda *lead: pltpu.VMEM(lead + tile, F32)
    sem = lambda n: pltpu.SemaphoreType.DMA((n,))
    vspec = pl.BlockSpec(memory_space=pltpu.VMEM)
    return pl.pallas_call(
        tail_kernel,
        in_specs=[vspec, vspec, pl.BlockSpec(memory_space=pl.ANY)],
        out_specs=vspec,
        out_shape=jax.ShapeDtypeStruct((128, 512), F32),
        scratch_shapes=[pltpu.VMEM((8, NB, 512), jnp.bfloat16)]
        + [vm(2, 4, 4, 4, n) for n in MAIN_N]
        + [vm(4, 4, 4, n) for n in MAIN_N]
        + [vm(3, 4, 4, n) for n in MAIN_N]
        + [vm(3, 4, n) for n in MAIN_N]
        + [
            vm(3, 16), vm(4, 16), pltpu.VMEM((512, 512), F32),
            vm(2, 80), vm(80), vm(80), vm(3, 20), vm(3, 5), vm(3, 5), vm(2, 80),
            pltpu.VMEM((512, 512), F32), pltpu.VMEM((4, 128, 128), F32),
            sem(8), sem(24), sem(24), pltpu.SemaphoreType.DMA, pltpu.SemaphoreType.DMA,
            sem(27), sem(27), sem(27), sem(27), sem(22), sem(22),
        ],
        compiler_params=pltpu.CompilerParams(
            collective_id=0, has_side_effects=True, vmem_limit_bytes=56 << 20
        ),
    )(hess, solved_t, coupling)


def per_device(coupling, scen_kkt, active_rows, first_hess):
    solved_t = scenario_solve(active_rows, scen_kkt[0], coupling[0])
    return tail(first_hess.reshape(4, 128), solved_t, coupling[0])


def solution(mesh):
    placed = (
        P(("scen", "grp"), None, None),
        P(("scen", "grp"), None, None),
        P(("scen", "grp")),
        P(),
    )
    return jax.shard_map(
        per_device, mesh=mesh, in_specs=placed, out_specs=P("scen", None), check_vma=False
    )
```

time: 159 us -> 138 us (0.87)
  Pallas kernels: 156 us -> 132 us
  local copies, waits for them, and re-layouts: 1.27 us -> 3.81 us
    pallas_call x3 -> x1, Pallas kernels: 102 us -> 78.6 us  [tail(): pl.pallas_call(tail_kernel, in_specs=[vspec, vspec, pl.BlockSpec(memory_s...]
    unnamed x4 -> x5, local copies, waits for them, and re-layouts: 1.27 us -> 3.81 us
where the time goes in v1:
time: 138 us; the launch traced here: 137 us
  Pallas kernels  132 us (96%)
  local copies, waits for them, and re-layouts  3.81 us (3%)
    pallas_call x1, Pallas kernels, tail(): pl.pallas_call(tail_kernel, in_specs=[vspec, vspec, pl.BlockSpec(memory_s...  78.6 us
    pallas_call x1, Pallas kernels, scenario_solve(): pl.pallas_call(solve_kernel, grid=(1,), in_specs=[pl.BlockSpec(memory_spa...  53.5 us
    unnamed x5, local copies, waits for them, and re-layouts  3.81 us

profile of v1, /device:TPU:0, one launch (start us, length us, event | category | flops | bytes accessed | tf_op | source)
XLA Modules:
  0.0 136.7 jit_solution(15745410675564024105)
XLA Ops:
  0.7 0.0 copy-start.1
  0.7 1.3 copy-done.1
  1.9 53.5 %shard_map.46.st_ref = bf16[512,768]{1,0:T(8,128)(2,1)S(1)} custom-call(s32[1]{0:T(128)S(6)} %copy.6.act_ref, bf16[768,768]{1,0:T(8,128)(2,1)S(1)} %bitcast.3, bf16[768,4096]{1,0:T(8,128)(2,1)} %bitcast.4), custom_call_target="tpu_custom_call" | custom-call | tf_op jit(solution)/shard_map/pallas_call | solution.py:108
  55.5 0.0 copy-start
  55.5 0.9 copy-done
  56.3 78.6 %shard_map.47 = f32[128,512]{1,0:T(8,128)} custom-call(f32[4,128]{1,0:T(4,128)} %bitcast.6, bf16[512,768]{1,0:T(8,128)(2,1)} %copy-done, bf16[768,4096]{1,0:T(8,128)(2,1)} %bitcast.5), custom_call_target="tpu_custom_call" | custom-call | tf_op jit(solution)/shard_map/pallas_call | solution.py:443
  135.0 1.7 %copy.7 = f32[128,512]{1,0:T(8,128)} copy(f32[128,512]{1,0:T(8,128)} %shard_map.47) | data formatting | bytes 524288
Async XLA Ops:
  0.7 1.3 copy-start.1
  55.5 0.9 copy-start

commit v2 on v1

--- a/solution.py
+++ b/solution.py
@@ -355,14 +355,10 @@
         chunk_add(i)
     top_total()
     top_gather(1)
-    if EARLY_ROWS:
-        for k in range(3):
-            row_scatter(0, k)
     top_wait()
     top_gather(0)
-    if not EARLY_ROWS:
-        for k in range(3):
-            row_scatter(0, k)
+    for k in range(3):
+        row_scatter(0, k)
     top_wait()
     tlast = send(gat.at[c], gat.at[c], ag_s.at[18], ag_r.at[18], partner)
     tlast.wait_recv()
@@ -376,11 +372,17 @@
         aug[a * 128 : (a + 1) * 128, b * 128 : (b + 1) * 128] = v
 
     def step(j, _):
-        @pl.when(j == 3)
+        @pl.when(j == 2)
         def _():
             for k in range(3):
                 row_sum(0, k)
                 row_scatter(1, k)
+
+        @pl.when(j == 3)
+        def _():
+            for k in range(3):
+                row_sum(1, k)
+                row_scatter(2, k)
 
         at = pl.multiple_of(j * 128, 128)
         rows = pl.ds(at, 128)
@@ -400,9 +402,6 @@
         return 0
 
     lax.fori_loop(0, 4, step, 0)
-    for k in range(3):
-        row_sum(1, k)
-        row_scatter(2, k)
     for k in range(3):
         row_sum(2, k)
     mine = own.at[gi]
@@ -430,9 +429,6 @@
         for k in range(3):
             for d in (1, 2, 3):
                 row_copy(stage, k, d).wait_send()
-
-
-EARLY_ROWS = True
 
 
 def tail(hess, solved_t, coupling):

time: 138 us -> 125 us (0.906)
  Pallas kernels: 132 us -> 119 us
    pallas_call x1, Pallas kernels: 78.6 us -> 65.9 us  [tail(): pl.pallas_call(tail_kernel, in_specs=[vspec, vspec, pl.BlockSpec(memory_s...]
where the time goes in v2:
time: 125 us; the launch traced here: 124 us
  Pallas kernels  119 us (95%)
  local copies, waits for them, and re-layouts  3.81 us (3%)
    pallas_call x1, Pallas kernels, tail(): pl.pallas_call(tail_kernel, in_specs=[vspec, vspec, pl.BlockSpec(memory_s...  65.9 us
    pallas_call x1, Pallas kernels, scenario_solve(): pl.pallas_call(solve_kernel, grid=(1,), in_specs=[pl.BlockSpec(memory_spa...  53.5 us
    unnamed x5, local copies, waits for them, and re-layouts  3.81 us

profile of v2, /device:TPU:0, one launch (start us, length us, event | category | flops | bytes accessed | tf_op | source)
XLA Modules:
  0.0 123.9 jit_solution(7549185943148988664)
XLA Ops:
  0.7 0.0 copy-start.1
  0.7 1.3 %copy-done.1 = bf16[1,768,768]{2,1,0:T(8,128)(2,1)S(1)} copy-done((bf16[1,768,768]{2,1,0:T(8,128)(2,1)S(1)}, bf16[1,768,768]{2,1,0:T(8,128)(2,1)}, u32[]{:S(2)}) %copy-start.1) | copy-done | bytes 1179672
  1.9 53.5 %shard_map.46.st_ref = bf16[512,768]{1,0:T(8,128)(2,1)S(1)} custom-call(s32[1]{0:T(128)S(6)} %copy.6.act_ref, bf16[768,768]{1,0:T(8,128)(2,1)S(1)} %bitcast.3, bf16[768,4096]{1,0:T(8,128)(2,1)} %bitcast.4), custom_call_target="tpu_custom_call" | custom-call | tf_op jit(solution)/shard_map/pallas_call | solution.py:108
  55.5 0.0 copy-start
  55.5 0.9 copy-done
  56.3 65.9 %shard_map.47 = f32[128,512]{1,0:T(8,128)} custom-call(f32[4,128]{1,0:T(4,128)} %bitcast.6, bf16[512,768]{1,0:T(8,128)(2,1)} %copy-done, bf16[768,4096]{1,0:T(8,128)(2,1)} %bitcast.5), custom_call_target="tpu_custom_call" | custom-call | tf_op jit(solution)/shard_map/pallas_call | solution.py:439
  122.2 1.7 %copy.7 = f32[128,512]{1,0:T(8,128)} copy(f32[128,512]{1,0:T(8,128)} %shard_map.47) | data formatting | bytes 524288
Async XLA Ops:
  0.7 1.3 %copy-start.1 = (bf16[1,768,768]{2,1,0:T(8,128)(2,1)S(1)}, bf16[1,768,768]{2,1,0:T(8,128)(2,1)}, u32[]{:S(2)}) copy-start(bf16[1,768,768]{2,1,0:T(8,128)(2,1)} %param.5) | copy-start | bytes 3538948
  55.5 0.9 copy-start

commit v3 on v2

--- a/solution.py
+++ b/solution.py
@@ -9,7 +9,6 @@
 NC = 4096
 NB = 768
 F32 = jnp.float32
-HIGHEST = lax.Precision.HIGHEST
 MESH = pl.DeviceIdType.MESH
 
 ORDERS = (("x", "y", "z"), ("y", "z", "x"), ("z", "x", "y"))
@@ -23,6 +22,30 @@
     while len(terms) > 1:
         terms = [terms[i] + terms[i + 1] if i + 1 < len(terms) else terms[i] for i in range(0, len(terms), 2)]
     return terms[0]
+
+def pair_factor(e):
+    inv, l, t = {}, {}, {}
+    for c in range(0, 8, 2):
+        d = c + 1
+        a = e[c, c]
+        b = e[d, c]
+        ra = lax.rsqrt(a)
+        rd = lax.rsqrt(a * e[d, d] - b * b)
+        inv[c] = ra
+        inv[d] = (a * ra) * rd
+        l[d, c] = b * ra
+        for r in range(c + 2, 8):
+            l[r, c] = e[r, c] * ra
+            l[r, d] = (e[r, d] - l[r, c] * l[d, c]) * inv[d]
+        for r in range(c + 2, 8):
+            for q in range(c + 2, r + 1):
+                e[r, q] = (e[r, q] - l[r, c] * l[q, c]) - l[r, d] * l[q, d]
+    return inv, l
+
+
+def bc(x, r):
+    return jnp.broadcast_to(x[r : r + 1, :], (8, 128))
+
 
 def inverse_factor(z):
     shape = (8, 128)
@@ -32,23 +55,18 @@
     for j in range(16):
         lo = 8 * j
         zj = z[j]
-        col = [jnp.broadcast_to(zj[:, lo + c : lo + c + 1], shape) for c in range(8)]
-        e = {(r, c): jnp.broadcast_to(col[c][r : r + 1], shape) for c in range(8) for r in range(c, 8)}
-        inv, l, t = {}, {}, {}
-        for c in range(8):
-            inv[c] = lax.rsqrt(e[c, c])
-            for r in range(c + 1, 8):
-                l[r, c] = e[r, c] * inv[c]
-            for r in range(c + 1, 8):
-                for q in range(c + 1, r + 1):
-                    e[r, q] = e[r, q] - l[r, c] * l[q, c]
+        panel = (lane >= lo) & (lane < lo + 8)
+        zp = jnp.where(panel, jnp.where(lane - lo == sub, 1.0, 0.0), zj)
+        rows = [bc(zj, r) for r in range(8)]
+        zero = jnp.zeros(shape, F32)
+        e = {(r, c): jnp.broadcast_to((rows[r] + zero)[:, lo + c : lo + c + 1], shape) for c in range(8) for r in range(c, 8)}
+        inv, l = pair_factor(e)
+        t = {}
         for c in range(8):
             t[c, c] = inv[c]
             for r in range(c + 1, 8):
                 t[r, c] = -inv[r] * total([l[r, m] * t[m, c] for m in range(c, r)])
-        panel = (lane >= lo) & (lane < lo + 8)
-        zp = jnp.where(panel, jnp.where(lane - lo == sub, 1.0, 0.0), zj)
-        zb = [jnp.broadcast_to(zp[c : c + 1], shape) for c in range(8)]
+        zb = [bc(zp, c) for c in range(8)]
         u = [total([t[r, c] * zb[c] for c in range(r + 1)]) for r in range(8)]
         w = [total([t[c, r] * u[c] for c in range(r, 8)]) for r in range(8)]
         row = u[0]
@@ -61,13 +79,28 @@
             z[i] = jnp.where(panel, 0.0, zi) - total(q)
     return z
 
+
+BF16 = jnp.bfloat16
+
+def halves(a):
+    hi = a.astype(BF16)
+    return hi, (a - hi.astype(F32)).astype(BF16)
+
+def left(a, axis):
+    hi, lo = halves(a)
+    return jnp.concatenate([hi, lo, hi], axis)
+
+def right(a):
+    hi, lo = halves(a)
+    return jnp.concatenate([hi, hi, lo], 0)
+
 def dot(a, b):
-    return jnp.dot(a, b, precision=HIGHEST, preferred_element_type=F32)
+    return jnp.dot(left(a, 1), right(b), preferred_element_type=F32)
 
 def dot_t(a, b):
-    return lax.dot_general(a, b, (((0,), (0,)), ((), ())), precision=HIGHEST, preferred_element_type=F32)
-
-def solve_kernel(act_ref, k_ref, c_ref, st_ref, aug, linv, xs):
+    return lax.dot_general(left(a, 0), right(b), (((0,), (0,)), ((), ())), preferred_element_type=F32)
+
+def solve_kernel(act_ref, k_ref, c_ref, st_ref, aug, linv, xs, yl, yr):
     row = lax.broadcasted_iota(jnp.int32, (NB, 1), 0)
     keep = (row < act_ref[0]).astype(F32)
     aug[:, :NB] = k_ref[...].astype(F32)
@@ -82,12 +115,20 @@
             linv[j, 8 * i : 8 * i + 8, :] = z[i]
         y = dot(linv[j], aug[rows, :])
         aug[rows, :] = y
+        hi, lo = halves(y)
+        yl[0:128] = hi[:, :NB]
+        yl[128:256] = lo[:, :NB]
+        yl[256:384] = hi[:, :NB]
+        yr[0:128] = hi
+        yr[128:256] = hi
+        yr[256:384] = lo
 
         def update(i, _):
             ai = pl.multiple_of(i * 128, 128)
-            g = aug[rows, pl.ds(ai, 128)]
             below = pl.ds(ai, 128)
-            aug[below, :] = aug[below, :] - dot_t(g, aug[rows, :])
+            aug[below, :] = aug[below, :] - lax.dot_general(
+                yl[:, pl.ds(ai, 128)], yr[...], (((0,), (0,)), ((), ())), preferred_element_type=F32
+            )
             return 0
 
         lax.fori_loop(j + 1, NB // 128, update, 0)
@@ -112,7 +153,8 @@
                   pl.BlockSpec((NB, 512), lambda i: (0, 0))],
         out_specs=pl.BlockSpec((512, NB), lambda i: (0, 0)),
         out_shape=jax.ShapeDtypeStruct((512, NB), jnp.bfloat16),
-        scratch_shapes=[pltpu.VMEM((NB, 1280), F32), pltpu.VMEM((6, 128, 128), F32), pltpu.VMEM((NB, 512), F32)],
+        scratch_shapes=[pltpu.VMEM((NB, 1280), F32), pltpu.VMEM((6, 128, 128), F32), pltpu.VMEM((NB, 512), F32),
+                        pltpu.VMEM((384, NB), BF16), pltpu.VMEM((384, 1280), BF16)],
         compiler_params=pltpu.CompilerParams(vmem_limit_bytes=48 << 20),
     )(active, kkt, coupling)
 
@@ -123,7 +165,7 @@
 def tail_kernel(
     hess_ref, st_ref, coup_ref, out_ref,
     cbuf, ma, mb, mc, ra, rb, rc, pa, pb, pc, qa, qb, qc, last_slots, own,
-    keep, top, tacc, ta, t0, t1, t2, gat, aug, linv,
+    keep, top, tacc, ta, t0, t1, t2, gat, aug, linv, sol,
     c_sem, core_s, core_r, tcore_s, tcore_r, st_s, st_r, tst_s, tst_r, ag_s, ag_r,
 ):
     si = lax.axis_index("scen")
@@ -412,15 +454,15 @@
     for cp in flights:
         cp.wait_recv()
 
-    solved = []
     for j in range(4):
+        lo, hi = j * 128, j * 128 + 128
         acc = own[j].reshape(128, 128)
-        for i in range(j):
-            acc = acc - dot_t(aug[i * 128 : (i + 1) * 128, j * 128 : (j + 1) * 128], solved[i])
-        solved.append(dot(linv[j], acc))
+        if j:
+            acc = acc - dot_t(aug[:lo, lo:hi], sol[:lo, :])
+        sol[lo:hi, :] = dot(linv[j], acc)
     at = pl.multiple_of(jnp.where(si < 4, si, 0) * 128, 128)
     for j in range(4):
-        v = jnp.where(si < 4, aug[j * 128 : (j + 1) * 128, pl.ds(at, 128)], solved[j])
+        v = jnp.where(si < 4, aug[j * 128 : (j + 1) * 128, pl.ds(at, 128)], sol[j * 128 : (j + 1) * 128, :])
         v = jnp.where(j * 128 + row <= si * 128 + lane, v, 0.0)
         out_ref[:, j * 128 : (j + 1) * 128] = v.T
     for cp in pending:
@@ -450,6 +492,7 @@
             vm(3, 16), vm(4, 16), pltpu.VMEM((512, 512), F32),
             vm(2, 80), vm(80), vm(80), vm(3, 20), vm(3, 5), vm(3, 5), vm(2, 80),
             pltpu.VMEM((512, 512), F32), pltpu.VMEM((4, 128, 128), F32),
+            pltpu.VMEM((512, 128), F32),
             sem(8), sem(24), sem(24), pltpu.SemaphoreType.DMA, pltpu.SemaphoreType.DMA,
             sem(27), sem(27), sem(27), sem(27), sem(22), sem(22),
         ],

time: 125 us -> 98.5 us (0.79)
  Pallas kernels: 119 us -> 92.4 us
    pallas_call x1, Pallas kernels: 53.5 us -> 31.7 us  [scenario_solve(): pl.pallas_call(solve_kernel, grid=(1,), in_specs=[pl.BlockSpec(memory_spa...]
    pallas_call x1, Pallas kernels: 65.9 us -> 60.7 us  [tail(): pl.pallas_call(tail_kernel, in_specs=[vspec, vspec, pl.BlockSpec(memory_s...]
where the time goes in v3:
time: 98.5 us; the launch traced here: 96.9 us
  Pallas kernels  92.4 us (94%)
  local copies, waits for them, and re-layouts  3.81 us (4%)
    pallas_call x1, Pallas kernels, tail(): pl.pallas_call(tail_kernel, in_specs=[vspec, vspec, pl.BlockSpec(memory_s...  60.7 us
    pallas_call x1, Pallas kernels, scenario_solve(): pl.pallas_call(solve_kernel, grid=(1,), in_specs=[pl.BlockSpec(memory_spa...  31.7 us
    unnamed x5, local copies, waits for them, and re-layouts  3.81 us

profile of v3, /device:TPU:0, one launch (start us, length us, event | category | flops | bytes accessed | tf_op | source)
XLA Modules:
  0.0 96.9 jit_solution(15852572372769215458)
XLA Ops:
  0.7 0.0 copy-start.1
  0.7 1.3 %copy-done.1 = bf16[1,768,768]{2,1,0:T(8,128)(2,1)S(1)} copy-done((bf16[1,768,768]{2,1,0:T(8,128)(2,1)S(1)}, bf16[1,768,768]{2,1,0:T(8,128)(2,1)}, u32[]{:S(2)}) %copy-start.1) | copy-done | bytes 1179672
  1.9 31.7 %shard_map.46.st_ref = bf16[512,768]{1,0:T(8,128)(2,1)S(1)} custom-call(s32[1]{0:T(128)S(6)} %copy.6.act_ref, bf16[768,768]{1,0:T(8,128)(2,1)S(1)} %bitcast.3, bf16[768,4096]{1,0:T(8,128)(2,1)} %bitcast.4), custom_call_target="tpu_custom_call" | custom-call | tf_op jit(solution)/shard_map/pallas_call | solution.py:149
  33.6 0.0 copy-start
  33.6 0.9 copy-done
  34.5 60.7 %shard_map.47 = f32[128,512]{1,0:T(8,128)} custom-call(f32[4,128]{1,0:T(4,128)} %bitcast.6, bf16[512,768]{1,0:T(8,128)(2,1)} %copy-done, bf16[768,4096]{1,0:T(8,128)(2,1)} %bitcast.5), custom_call_target="tpu_custom_call" | custom-call | tf_op jit(solution)/shard_map/pallas_call | solution.py:481
  95.2 1.7 %copy.7 = f32[128,512]{1,0:T(8,128)} copy(f32[128,512]{1,0:T(8,128)} %shard_map.47) | data formatting | bytes 524288
Async XLA Ops:
  0.7 1.3 %copy-start.1 = (bf16[1,768,768]{2,1,0:T(8,128)(2,1)S(1)}, bf16[1,768,768]{2,1,0:T(8,128)(2,1)}, u32[]{:S(2)}) copy-start(bf16[1,768,768]{2,1,0:T(8,128)(2,1)} %param.5) | copy-start | bytes 3538948
  33.6 0.9 copy-start

commit v4 on v3

v4 whole, which is shorter than its diff:
```python
import jax
import jax.numpy as jnp
from jax import lax
from jax.experimental import pallas as pl
from jax.experimental.pallas import tpu as pltpu
from jax.sharding import PartitionSpec as P

PW = 256
NC = 4096
NB = 768
F32 = jnp.float32
MESH = pl.DeviceIdType.MESH

ORDERS = (("x", "y", "z"), ("y", "z", "x"), ("z", "x", "y"))
MAIN_N = (5, 5, 6)
MAIN_OFF = (0, 5, 10)
HOOKS = (2, 3)
TOP_N = (4, 4, 2)
TOP_OFF = (0, 64, 128)


def total(terms):
    while len(terms) > 1:
        terms = [terms[i] + terms[i + 1] if i + 1 < len(terms) else terms[i] for i in range(0, len(terms), 2)]
    return terms[0]

def pair_factor(e):
    inv, l, t = {}, {}, {}
    for c in range(0, 8, 2):
        d = c + 1
        a = e[c, c]
        b = e[d, c]
        ra = lax.rsqrt(a)
        rd = lax.rsqrt(a * e[d, d] - b * b)
        inv[c] = ra
        inv[d] = (a * ra) * rd
        l[d, c] = b * ra
        for r in range(c + 2, 8):
            l[r, c] = e[r, c] * ra
            l[r, d] = (e[r, d] - l[r, c] * l[d, c]) * inv[d]
        for r in range(c + 2, 8):
            for q in range(c + 2, r + 1):
                e[r, q] = (e[r, q] - l[r, c] * l[q, c]) - l[r, d] * l[q, d]
    return inv, l


def bc(x, r):
    return jnp.broadcast_to(x[r : r + 1, :], (8, 128))


def inverse_factor(z):
    shape = (8, 128)
    lane = lax.broadcasted_iota(jnp.int32, shape, 1)
    sub = lax.broadcasted_iota(jnp.int32, shape, 0)
    z = list(z)
    for j in range(16):
        lo = 8 * j
        zj = z[j]
        panel = (lane >= lo) & (lane < lo + 8)
        zp = jnp.where(panel, jnp.where(lane - lo == sub, 1.0, 0.0), zj)
        rows = [bc(zj, r) for r in range(8)]
        zero = jnp.zeros(shape, F32)
        e = {(r, c): jnp.broadcast_to((rows[r] + zero)[:, lo + c : lo + c + 1], shape) for c in range(8) for r in range(c, 8)}
        inv, l = pair_factor(e)
        t = {}
        for c in range(8):
            t[c, c] = inv[c]
            for r in range(c + 1, 8):
                t[r, c] = -inv[r] * total([l[r, m] * t[m, c] for m in range(c, r)])
        zb = [bc(zp, c) for c in range(8)]
        u = [total([t[r, c] * zb[c] for c in range(r + 1)]) for r in range(8)]
        w = [total([t[c, r] * u[c] for c in range(r, 8)]) for r in range(8)]
        row = u[0]
        for r in range(1, 8):
            row = jnp.where(sub == r, u[r], row)
        z[j] = jnp.where(lane < lo + 8, row, 0.0)
        for i in range(j + 1, 16):
            zi = z[i]
            q = [jnp.broadcast_to(zi[:, lo + c : lo + c + 1], shape) * w[c] for c in range(8)]
            z[i] = jnp.where(panel, 0.0, zi) - total(q)
    return z


BF16 = jnp.bfloat16

def halves(a):
    hi = a.astype(BF16)
    return hi, (a - hi.astype(F32)).astype(BF16)

def left(a, axis):
    hi, lo = halves(a)
    return jnp.concatenate([hi, lo, hi], axis)

def right(a):
    hi, lo = halves(a)
    return jnp.concatenate([hi, hi, lo], 0)

def dot(a, b):
    return jnp.dot(left(a, 1), right(b), preferred_element_type=F32)

def dot_t(a, b):
    return lax.dot_general(left(a, 0), right(b), (((0,), (0,)), ((), ())), preferred_element_type=F32)

UPPER = ((0, 0), (0, 1), (1, 1), (0, 2), (1, 2), (0, 3), (1, 3), (2, 2), (2, 3), (3, 3))


def step_kernel(
    act_ref, hess_ref, kkt_ref, coup_ref, out_ref,
    kbuf, big, blinv, xs, yl, yr, stop, st_ref, tinv, tl,
    cbuf, ma, mb, mc, ra, rb, rc, pa, pb, pc, qa, qb, qc, last_slots, own,
    top, tacc, ta, t0, t1, t2, gat, aug, linv,
    k_sem, c_sem, core_s, core_r, tcore_s, tcore_r, tback_s, tback_r, st_s, st_r, tst_s, tst_r, ag_s, ag_r,
):
    si = lax.axis_index("scen")
    gi = lax.axis_index("grp")
    c = gi % 2
    zh = gi // 2
    pos = {"y": si // 8, "x": (si // 2) % 4, "z": 2 * zh + si % 2}
    main, recv_core = (ma, mb, mc), (ra, rb, rc)
    slots = ((pa, pb, pc), (qa, qb, qc))

    kload = pltpu.make_async_copy(kkt_ref, kbuf, k_sem)
    kload.start()
    loads = [
        pltpu.make_async_copy(coup_ref.at[:, pl.ds(i * 512, 512)], cbuf.at[i], c_sem.at[i])
        for i in range(8)
    ]
    for cp in loads:
        cp.start()

    def device(y, x, z, core):
        return {"scen": (y * 4 + x) * 2 + z % 2, "grp": (z // 2) * 2 + core}

    def peer(axis, dist):
        at = dict(pos)
        at[axis] = (at[axis] + dist) % 4
        return device(at["y"], at["x"], at["z"], c)

    partner = device(pos["y"], pos["x"], pos["z"], 1 - c)
    far = device(pos["y"], pos["x"], (pos["z"] + 2) % 4, 1 - c)

    barrier = pltpu.get_barrier_semaphore()
    greet = [peer(a, d) for a in "xyz" for d in (1, 2, 3)] + [partner, far]
    for dev in greet:
        pl.semaphore_signal(barrier, inc=1, device_id=dev, device_id_type=MESH)

    def meet():
        pl.semaphore_wait(barrier, len(greet))

    pending = []

    def send(src, dst, ssem, rsem, dev):
        cp = pltpu.make_async_remote_copy(
            src_ref=src, dst_ref=dst, send_sem=ssem, recv_sem=rsem,
            device_id=dev, device_id_type=MESH,
        )
        cp.start()
        pending.append(cp)
        return cp

    chunk_flights = []

    def region(k, y, x0):
        at = {"x": pl.ds(x0, 2), "y": y, "z": pl.ds(0, 4)}
        return tuple(at[a] for a in ORDERS[k])

    def chunk(i):
        y, x0 = i // 2, (i % 2) * 2
        if i:
            loads[i].wait()
        res = jnp.dot(st_ref[...], cbuf[i], preferred_element_type=F32)
        for t in range(4):
            x, zl = x0 + t // 2, t % 2
            part = res[:, t * 128 : (t + 1) * 128]
            for q in range(4):
                at = {"x": x, "y": y, "z": 2 * (q // 2) + zl}
                for k in range(3):
                    n = MAIN_N[k]
                    lo = q * 128 + MAIN_OFF[k] * 8
                    i0, i1, i2 = (at[a] for a in ORDERS[k])
                    main[k][q % 2, i0, i1, i2] = part[lo : lo + 8 * n].reshape(n, 8, 128)

    def chunk_send(i):
        y, x0 = i // 2, (i % 2) * 2
        out = []
        for k in range(3):
            r = region(k, y, x0)
            out.append(
                send(main[k].at[(1 - c,) + r], recv_core[k].at[r],
                     core_s.at[i * 3 + k], core_r.at[i * 3 + k], partner)
            )
        chunk_flights.append(out)

    def chunk_add(i):
        y, x0 = i // 2, (i % 2) * 2
        for k in range(3):
            chunk_flights[i][k].wait_recv()
            r = region(k, y, x0)
            main[k][(c,) + r] = main[k][(c,) + r] + recv_core[k][r]

    def top_tiles():
        for i, (a, b) in enumerate(UPPER):
            v = stop[a * 128 : (a + 1) * 128, b * 128 : (b + 1) * 128]
            top[i * 16 : i * 16 + 16] = v.reshape(16, 8, 128)

    def add_top():
        for a in range(4):
            lo, hi = a * 128, a * 128 + 128
            stop[lo:hi, lo:] += lax.dot_general(
                yl[:, NB + lo : NB + hi], yr[:, NB + lo :], (((0,), (0,)), ((), ())),
                preferred_element_type=F32,
            )

    def forward(j, _):
        at = pl.multiple_of(j * 128, 128)
        rows = pl.ds(at, 128)
        z = [big[pl.ds(at + 8 * i, 8), pl.ds(at, 128)] for i in range(16)]
        add_top()
        z = inverse_factor(z)
        for i in range(16):
            blinv[j, 8 * i : 8 * i + 8, :] = z[i]
        y = dot(blinv[j], big[rows, :])
        big[rows, :] = y
        hi, lo = halves(y)
        yl[0:128] = hi
        yl[128:256] = lo
        yl[256:384] = hi
        yr[0:128] = hi
        yr[128:256] = hi
        yr[256:384] = lo

        def update(i, _):
            ai = pl.multiple_of(i * 128, 128)
            below = pl.ds(ai, 128)
            big[below, :] = big[below, :] - lax.dot_general(
                yl[:, pl.ds(ai, 128)], yr[...], (((0,), (0,)), ((), ())), preferred_element_type=F32
            )
            return 0

        lax.fori_loop(j + 1, NB // 128, update, 0)
        return 0

    def backward(*blocks):
        for j in blocks:
            lo, hi = j * 128, j * 128 + 128
            acc = big[lo:hi, NB:]
            if hi < NB:
                acc = acc - dot(big[lo:hi, hi:NB], xs[hi:, :])
            x = dot_t(blinv[j], acc)
            xs[lo:hi, :] = x
            st_ref[:, lo:hi] = (x * kept(lo, hi)).T.astype(BF16)

    def kept(lo, hi):
        row = lax.broadcasted_iota(jnp.int32, (hi - lo, 1), 0) + lo
        return (row < act_ref[0]).astype(F32)

    def remote(src, dst, ssem, rsem, dev):
        return pltpu.make_async_remote_copy(
            src_ref=src, dst_ref=dst, send_sem=ssem, recv_sem=rsem,
            device_id=dev, device_id_type=MESH,
        )

    def to_core_0():
        return remote(top, ta, tcore_s, tcore_r, partner)

    def to_core_1():
        return remote(gat, gat, tback_s, tback_r, partner)

    def top_base(k, stage):
        base = TOP_OFF[k]
        if stage >= 1:
            base = base + pos[ORDERS[k][0]] * (4 * TOP_N[k])
        if stage >= 2:
            base = base + pos[ORDERS[k][1]] * TOP_N[k]
        return base

    def top_copy(stage, k, d):
        axis = ORDERS[k][(0, 1, 2, 1, 0)[stage]]
        n = TOP_N[k] * (4 if stage in (0, 4) else 1)
        if stage < 2:
            src = tacc.at[pl.ds(top_base(k, stage) + (pos[axis] + d) % 4 * n, n)]
            dst = (t0, t1)[stage].at[d - 1, pl.ds(TOP_OFF[k] // (4, 16)[stage], n)]
        elif stage == 2:
            src = tacc.at[pl.ds(top_base(k, 2), n)]
            dst = t2.at[d - 1, pl.ds(TOP_OFF[k] // 16, n)]
        else:
            src = dst = gat.at[pl.ds(top_base(k, 5 - stage), n)]
        i = (stage * 3 + k) * 3 + d - 1
        return remote(src, dst, tst_s.at[i], tst_r.at[i], peer(axis, d))

    def top_start(stage):
        for k in range(3):
            for d in (1, 2, 3):
                top_copy(stage, k, d).start()

    def top_wait(stage):
        for k in range(3):
            for d in (1, 2, 3):
                top_copy(stage, k, d).wait_recv()

    def top_sum(stage):
        got = (t0, t1)[stage]
        top_wait(stage)
        for k in range(3):
            n = TOP_N[k] * (4, 1)[stage]
            mine, sl = pl.ds(top_base(k, stage + 1), n), pl.ds(TOP_OFF[k] // (4, 16)[stage], n)
            tacc[mine] = (tacc[mine] + got[0, sl]) + (got[1, sl] + got[2, sl])

    def top_total():
        top_wait(2)
        for k in range(3):
            n, off, mine = TOP_N[k], TOP_OFF[k] // 16, pos[ORDERS[k][2]]
            own_part = pl.ds(top_base(k, 2), n)
            parts = [tacc[own_part]] + [t2[d, pl.ds(off, n)] for d in range(3)]
            vals = []
            for p in range(4):
                dist = (mine - p) % 4
                vals.append(jnp.where(
                    dist == 0, parts[0],
                    jnp.where(dist == 1, parts[1], jnp.where(dist == 2, parts[2], parts[3])),
                ))
            gat[own_part] = (vals[0] + vals[1]) + (vals[2] + vals[3])

    def where(k, stage):
        return (c,) + tuple(pos[a] for a in ORDERS[k][:stage])

    def row_copy(stage, k, d):
        axis = ORDERS[k][stage]
        src = main[k].at[where(k, stage) + ((pos[axis] + d) % 4,)]
        dst = last_slots.at[d - 1, pl.ds(MAIN_OFF[k], MAIN_N[k])] if stage == 2 else slots[stage][k].at[d - 1]
        i = (stage * 3 + k) * 3 + d - 1
        return pltpu.make_async_remote_copy(
            src_ref=src, dst_ref=dst, send_sem=st_s.at[i], recv_sem=st_r.at[i],
            device_id=peer(axis, d), device_id_type=MESH,
        )

    def row_scatter(stage, k):
        for d in (1, 2, 3):
            row_copy(stage, k, d).start()

    def row_sum(stage, k):
        for d in (1, 2, 3):
            row_copy(stage, k, d).wait_recv()
        at = where(k, stage + 1)
        got = [
            last_slots[d, pl.ds(MAIN_OFF[k], MAIN_N[k])] if stage == 2 else slots[stage][k][d]
            for d in range(3)
        ]
        total_rows = (main[k][at] + got[0]) + (got[1] + got[2])
        if stage == 2:
            own[gi, pl.ds(MAIN_OFF[k], MAIN_N[k])] = total_rows
        else:
            main[k][at] = total_rows

    yl[...] = jnp.zeros_like(yl)
    yr[...] = jnp.zeros_like(yr)
    stop[...] = jnp.zeros_like(stop)
    kload.wait()
    big[:, :NB] = kbuf[...].astype(F32)
    loads[0].wait()
    big[:, NB:] = cbuf[0].astype(F32) * kept(0, NB)
    lax.fori_loop(0, NB // 128, forward, 0)
    add_top()
    top_tiles()
    meet()

    def product_and_core(*chunks):
        for i in chunks:
            chunk(i)
            chunk_send(i)

    first, second = c == 0, c == 1

    @pl.when(second)
    def _():
        to_core_0().start()

    backward(5)

    @pl.when(first)
    def _():
        to_core_0().wait_recv()
        tacc[...] = top[...] + ta[...]
        top_start(0)

    backward(4, 3, 2, 1)

    @pl.when(first)
    def _():
        top_sum(0)
        top_start(1)

    backward(0)
    product_and_core(0, 1, 2, 3)

    @pl.when(first)
    def _():
        top_sum(1)
        top_start(2)

    product_and_core(4, 5, 6, 7)

    @pl.when(first)
    def _():
        top_total()
        top_start(3)

    for i in range(8):
        chunk_add(i)

    @pl.when(second)
    def _():
        for k in range(3):
            row_scatter(0, k)
        to_core_1().wait_recv()

    @pl.when(first)
    def _():
        top_wait(3)
        top_start(4)
        for k in range(3):
            row_scatter(0, k)
        top_wait(4)
        to_core_1().start()

    row = lax.broadcasted_iota(jnp.int32, (128, 128), 0)
    lane = lax.broadcasted_iota(jnp.int32, (128, 128), 1)
    for i, (a, b) in enumerate(UPPER):
        v = gat[i * 16 : i * 16 + 16].reshape(128, 128)
        if a == b:
            v = v + jnp.where(row == lane, hess_ref[a : a + 1, :], 0.0)
        aug[a * 128 : (a + 1) * 128, b * 128 : (b + 1) * 128] = v

    def step(j, _):
        for stage, block in ((0, HOOKS[0]), (1, HOOKS[1])):
            @pl.when(j == block)
            def _():
                for k in range(3):
                    row_sum(stage, k)
                    row_scatter(stage + 1, k)

        at = pl.multiple_of(j * 128, 128)
        rows = pl.ds(at, 128)
        z = [aug[pl.ds(at + 8 * i, 8), pl.ds(at, 128)] for i in range(16)]
        z = inverse_factor(z)
        for i in range(16):
            linv[j, 8 * i : 8 * i + 8, :] = z[i]
        aug[rows, :] = dot(linv[j], aug[rows, :])

        def update(i, _):
            ai = pl.multiple_of(i * 128, 128)
            below = pl.ds(ai, 128)
            aug[below, :] = aug[below, :] - dot_t(aug[rows, pl.ds(ai, 128)], aug[rows, :])
            return 0

        lax.fori_loop(j + 1, 4, update, 0)
        return 0

    lax.fori_loop(0, 4, step, 0)

    for k in range(3):
        row_sum(2, k)

    mine = own.at[gi]
    flights = [
        send(mine, mine, ag_s.at[j], ag_r.at[j], dev)
        for j, dev in enumerate((partner, peer("z", 2), far))
    ]

    tinv[...] = jnp.zeros_like(tinv)
    for j in range(4):
        lo, hi = j * 128, j * 128 + 128
        if j:
            acc = dot_t(aug[:lo, lo:hi], tinv[:lo, :lo])
            tinv[lo:hi, :lo] = -dot(linv[j], acc)
        tinv[lo:hi, lo:hi] = linv[j]
    tl[...] = left(tinv[...], 1)

    for cp in flights:
        cp.wait_recv()

    sol = jnp.dot(tl[...], right(own[...].reshape(512, 128)), preferred_element_type=F32)
    at = pl.multiple_of(jnp.where(si < 4, si, 0) * 128, 128)
    for j in range(4):
        v = jnp.where(si < 4, aug[j * 128 : (j + 1) * 128, pl.ds(at, 128)], sol[j * 128 : (j + 1) * 128, :])
        v = jnp.where(j * 128 + row <= si * 128 + lane, v, 0.0)
        out_ref[:, j * 128 : (j + 1) * 128] = v.T
    for cp in pending:
        cp.wait_send()
    for stage in range(3):
        for k in range(3):
            for d in (1, 2, 3):
                row_copy(stage, k, d).wait_send()

    @pl.when(second)
    def _():
        to_core_0().wait_send()

    @pl.when(first)
    def _():
        to_core_1().wait_send()
        for stage in range(5):
            for k in range(3):
                for d in (1, 2, 3):
                    top_copy(stage, k, d).wait_send()


def whole_step(active, hess, kkt, coupling):
    tile = (8, 128)
    vm = lambda *lead: pltpu.VMEM(lead + tile, F32)
    sem = lambda n: pltpu.SemaphoreType.DMA((n,))
    vspec = pl.BlockSpec(memory_space=pltpu.VMEM)
    aspec = pl.BlockSpec(memory_space=pl.ANY)
    return pl.pallas_call(
        step_kernel,
        in_specs=[pl.BlockSpec(memory_space=pltpu.SMEM), vspec, aspec, aspec],
        out_specs=vspec,
        out_shape=jax.ShapeDtypeStruct((128, 512), F32),
        scratch_shapes=[
            pltpu.VMEM((NB, NB), BF16), pltpu.VMEM((NB, 1280), F32), pltpu.VMEM((6, 128, 128), F32),
            pltpu.VMEM((NB, 512), F32), pltpu.VMEM((384, 1280), BF16), pltpu.VMEM((384, 1280), BF16),
            pltpu.VMEM((512, 512), F32), pltpu.VMEM((512, NB), BF16), pltpu.VMEM((512, 512), F32),
            pltpu.VMEM((512, 1536), BF16), pltpu.VMEM((8, NB, 512), BF16),
        ]
        + [vm(2, 4, 4, 4, n) for n in MAIN_N]
        + [vm(4, 4, 4, n) for n in MAIN_N]
        + [vm(3, 4, 4, n) for n in MAIN_N]
        + [vm(3, 4, n) for n in MAIN_N]
        + [
            vm(3, 16), vm(4, 16),
            vm(160), vm(160), vm(160), vm(3, 40), vm(3, 10), vm(3, 10), vm(160),
            pltpu.VMEM((512, 512), F32), pltpu.VMEM((4, 128, 128), F32),
            pltpu.SemaphoreType.DMA, sem(8), sem(24), sem(24),
            pltpu.SemaphoreType.DMA, pltpu.SemaphoreType.DMA,
            pltpu.SemaphoreType.DMA, pltpu.SemaphoreType.DMA,
            sem(27), sem(27), sem(45), sem(45), sem(3), sem(3),
        ],
        compiler_params=pltpu.CompilerParams(
            collective_id=0, has_side_effects=True, vmem_limit_bytes=60 << 20
        ),
    )(active, hess, kkt, coupling)


def per_device(coupling, scen_kkt, active_rows, first_hess):
    return whole_step(active_rows, first_hess.reshape(4, 128), scen_kkt[0], coupling[0])


def solution(mesh):
    placed = (
        P(("scen", "grp"), None, None),
        P(("scen", "grp"), None, None),
        P(("scen", "grp")),
        P(),
    )
    return jax.shard_map(
        per_device, mesh=mesh, in_specs=placed, out_specs=P("scen", None), check_vma=False
    )
```

time: 98.5 us -> 96.1 us (0.976)
  local copies, waits for them, and re-layouts: 3.81 us -> 1.67 us
    unnamed x5 -> x1, local copies, waits for them, and re-layouts: 3.81 us -> 1.67 us
    pallas_call x2 -> x1, Pallas kernels: 92.4 us -> 92.4 us  [whole_step(): pl.pallas_call(step_kernel, in_specs=[pl.BlockSpec(memory_space=pltpu.SME...]
where the time goes in v4:
time: 96.1 us; the launch traced here: 94.7 us
  Pallas kernels  92.4 us (96%)
  local copies, waits for them, and re-layouts  1.67 us (2%)
    pallas_call x1, Pallas kernels, whole_step(): pl.pallas_call(step_kernel, in_specs=[pl.BlockSpec(memory_space=pltpu.SME...  92.4 us

profile of v4, /device:TPU:0, one launch (start us, length us, event | category | flops | bytes accessed | tf_op | source)
XLA Modules:
  0.0 94.7 jit_solution(17110327220360084647)
XLA Ops:
  0.7 92.4 %shard_map.46 = f32[128,512]{1,0:T(8,128)} custom-call(s32[1]{0:T(128)S(6)} %copy.6.act_ref, f32[4,128]{1,0:T(4,128)} %bitcast.5, bf16[768,768]{1,0:T(8,128)(2,1)} %bitcast.4, bf16[768,4096]{1,0:T(8,128)(2,1)} %bitcast.3), custom_call_target="tpu_custom_call" | custom-call | tf_op jit(solution)/shard_map/pallas_call | solution.py:514
  93.0 1.7 %copy.7 = f32[128,512]{1,0:T(8,128)} copy(f32[128,512]{1,0:T(8,128)} %shard_map.46) | data formatting | bytes 524288
